TPU v7x, 256 devices: a whole 4x4x8 slice. The times are simulated.
256 devices in a mesh: section: 8 (over x, core), dp: 32 (over y, z).
Axes of the slice: x: 4, y: 4, z: 8, core: 2. Of those that a mesh axis runs over, the one named last changes fastest.
Arguments:
- section_inputs: bfloat16 [8, 8, 1024, 8192], P('section', None, 'dp'), may hold values from -6 to 6
- adapter_down: bfloat16 [8, 8192, 128], P('section'), may hold values from -0.0625 to 0.0625
- adapter_up: bfloat16 [8, 8192, 128], P('section'), may hold values from -0.5 to 0.5
- representation: bfloat16 [8, 1024, 8192], P('section', 'dp'), may hold values from -6 to 6
- head_weights: bfloat16 [8192, 128], P('dp'), may hold values from -1 to 1
- head_targets: bfloat16 [8, 1024, 128], P('section', 'dp'), may hold values from -40 to 40
- head_task: int32 [8, 1], replicated, may hold values from 0 to 5
Outputs:
- down_grads: float32 [8, 8192, 128], P('section', 'dp')
- up_grads: float32 [8, 8192, 128], P('section', 'dp')
- task_weights: float32 [6], replicated
Inputs may be any that keep to these rules, and one draw needn't show every extreme that they name: `head_task`: each head belongs to one task, and every task has at least one head.
All inputs are finite; a program needn't handle non-finite values.
Results may differ from a plain program's by a relative error of at most 0.022.
Values may be sent and summed in bfloat16 or wider, within the bound.
No kernel may reach another device: no remote copies, remote signals or barrier semaphores. Data moves between devices by JAX's collectives and lax.ppermute only.
A program may use at most 64 MiB of HBM per device.

v0:
```python
import jax
import jax.numpy as jnp
from jax import lax
from jax.sharding import PartitionSpec as P

HEAD_OUT = 16
TASKS = 6
STEPS = 20
STEP_RATE = 3.0


def from_behind(value, axis, steps):
    count = lax.axis_size(axis)
    first, last = (max(0, -steps), min(count, count - steps))
    return lax.ppermute(value, axis, [(source, source + steps) for source in range(first, last)])


def swish_slope(preact):
    logistic = jax.nn.sigmoid(preact)
    return logistic * (1.0 + preact * (1.0 - logistic))


def section_back(inputs, down_map, up_map, cotangent):
    preact = jnp.dot(inputs, down_map, preferred_element_type=jnp.float32)
    active = jax.nn.silu(preact).astype(jnp.bfloat16)
    branch = jnp.dot(cotangent, up_map, preferred_element_type=jnp.float32)
    inner = (branch * swish_slope(preact)).astype(jnp.bfloat16)
    back = lax.dot_general(
        inner, down_map, (((1,), (1,)), ((), ())), preferred_element_type=jnp.float32
    )
    passed = (cotangent.astype(jnp.float32) + back).astype(jnp.bfloat16)
    return (active, inner, passed)


def store_row(buffer, value, index, valid):
    previous = lax.dynamic_index_in_dim(buffer, index, 0, keepdims=False)
    chosen = jnp.where(valid, value, previous)
    return lax.dynamic_update_index_in_dim(buffer, chosen, index, 0)


def descend(gram_matrix):
    trace_sum = jnp.trace(gram_matrix) + 1e-06
    start = jnp.full((TASKS,), 1.0 / TASKS, dtype=jnp.float32)

    def advance(counter, weights):
        descent = jnp.dot(gram_matrix, weights, precision=lax.Precision.HIGHEST) / trace_sum
        weights = weights * jnp.exp(-STEP_RATE * descent)
        return weights / jnp.sum(weights)

    return lax.fori_loop(0, STEPS, advance, start)


def body(
    section_inputs, adapter_down, adapter_up, representation, head_weights, head_targets, head_task
):
    sections = lax.axis_size("section")
    my_section = lax.axis_index("section")
    micro_count = section_inputs.shape[1]
    tok_rows = section_inputs.shape[2]
    dim_model = section_inputs.shape[3]
    rank_width = adapter_down.shape[2]
    saved = section_inputs[0]
    down_map = adapter_down[0]
    up_map = adapter_up[0]
    weights = lax.all_gather(head_weights, "dp", axis=0, tiled=True)
    predicted = jnp.dot(representation[0], weights, preferred_element_type=jnp.float32)
    residual = (predicted - head_targets[0].astype(jnp.float32)).astype(jnp.bfloat16)
    column_task = jnp.repeat(head_task[:, 0], HEAD_OUT)
    onehot = (column_task[None, :] == jnp.arange(TASKS, dtype=jnp.int32)[:, None]).astype(
        jnp.float32
    )
    masked = residual[None, :, :] * onehot.astype(jnp.bfloat16)[:, None, :]
    task_grads = jnp.einsum("atc,dc->atd", masked, weights, preferred_element_type=jnp.float32)
    partial_gram = jnp.einsum(
        "atd,btd->ab", task_grads, task_grads, precision=lax.Precision.HIGHEST
    )
    gram_matrix = lax.psum(partial_gram, ("section", "dp"))
    mixing = descend(gram_matrix)
    column_weight = jnp.dot(mixing, onehot, precision=lax.Precision.HIGHEST)
    weighted = (residual.astype(jnp.float32) * column_weight[None, :]).astype(jnp.bfloat16)
    own_grad = jnp.einsum(
        "tc,dc->td", weighted, weights, preferred_element_type=jnp.float32
    ).astype(jnp.bfloat16)
    cotangents = lax.all_gather(own_grad[None], "section", axis=0, tiled=True)

    def tick(counter, carry):
        incoming, grad_rows, active_rows, inner_rows = carry
        micro_index = counter - (sections - 1 - my_section)
        valid = (micro_index >= 0) & (micro_index < micro_count)
        clipped = jnp.clip(micro_index, 0, micro_count - 1)
        from_heads = lax.dynamic_index_in_dim(cotangents, clipped, 0, keepdims=False)
        current = jnp.where(my_section == sections - 1, from_heads, incoming)
        inputs = lax.dynamic_index_in_dim(saved, clipped, 0, keepdims=False)
        active, inner, passed = section_back(inputs, down_map, up_map, current)
        grad_rows = store_row(grad_rows, current, clipped, valid)
        active_rows = store_row(active_rows, active, clipped, valid)
        inner_rows = store_row(inner_rows, inner, clipped, valid)
        incoming = from_behind(passed, "section", -1)
        return (incoming, grad_rows, active_rows, inner_rows)

    start_carry = (
        jnp.zeros((tok_rows, dim_model), jnp.bfloat16),
        jnp.zeros((micro_count, tok_rows, dim_model), jnp.bfloat16),
        jnp.zeros((micro_count, tok_rows, rank_width), jnp.bfloat16),
        jnp.zeros((micro_count, tok_rows, rank_width), jnp.bfloat16),
    )
    finished = lax.fori_loop(0, micro_count + sections - 1, tick, start_carry)
    grad_rows = finished[1]
    active_rows = finished[2]
    inner_rows = finished[3]
    part_down = jnp.einsum("mtd,mtr->dr", saved, inner_rows, preferred_element_type=jnp.float32)
    part_up = jnp.einsum("mtd,mtr->dr", grad_rows, active_rows, preferred_element_type=jnp.float32)
    shares = lax.psum_scatter(
        jnp.concatenate([part_down, part_up], axis=1).astype(jnp.bfloat16),
        "dp",
        scatter_dimension=0,
        tiled=True,
    ).astype(jnp.float32)
    grad_down = shares[:, :rank_width]
    grad_up = shares[:, rank_width:]
    return (grad_down[None], grad_up[None], mixing)


def solution(mesh):
    in_specs = (
        P("section", None, "dp", None),
        P("section", None, None),
        P("section", None, None),
        P("section", "dp", None),
        P("dp", None),
        P("section", "dp", None),
        P(),
    )
    out_specs = (P("section", "dp", None), P("section", "dp", None), P())
    return jax.shard_map(body, mesh=mesh, in_specs=in_specs, out_specs=out_specs, check_vma=False)
```

profile of v0, /device:TPU:4, one launch (start us, length us, event | category | flops | bytes accessed | tf_op | source)
XLA Modules:
  0.0 765.6 jit_solution(4357182135453760184)
XLA Ops:
  8.8 82.9 %all-gather.4.cloned.1.call-done = bf16[8192,128]{1,0:T(8,128)(2,1)} async-done(((bf16[256,128]{1,0:T(8,128)(2,1)}), bf16[8192,128]{1,0:T(8,128)(2,1)}) %all-gather.4.cloned.1.call-update) | async-done | bytes 2097168 | tf_op jit(solution)/shard_map/all_gather | solution.py:65
  96.3 24.6 %fusion.22 = f32[6,6]{1,0:T(8,128)S(1)} fusion(f32[6,32,8192]{2,1,0:T(8,128)S(1)} %fusion.19), kind=kOutput, calls=%fused_computation.43 | convolution fusion | flops 113246208 | bytes 6291600 | tf_op jit(solution)/shard_map/atd,btd->ab/dot_general | solution.py:74
  120.9 72.7 %psum.7 = f32[6,6]{1,0:T(8,128)S(1)} all-reduce(f32[6,6]{1,0:T(8,128)S(1)} %fusion.22), channel_id=1, replica_groups=mesh['section'=8,'dp'=32] {'section','dp'}, use_global_device_ids=true, to_apply=%region_0.0 | all-reduce | flops 36 | bytes 288 | tf_op jit(solution)/shard_map/psum | solution.py:77
  194.8 28.4 %while.33 = (s32[]{:T(128)}, f32[6]{0:T(128)S(1)}, f32[6,6]{1,0:T(8,128)S(1)}, f32[]{:T(128)}, s32[]{:T(128)}, /*index=5*/s32[]{:T(128)}) while((s32[]{:T(128)}, f32[6]{0:T(128)S(1)}, f32[6,6]{1,0:T(8,128)S(1)}, f32[]{:T(128)}, s32[]{:T(128)}, /*index=5*/s32[]{:T(128)}) %tuple.73), condition=%wide.region_4.5_spmd.clone, body=%wide.region_2.4_spmd.clone.sunk | while | flops 476 | bytes 331 | solution.py:50
  226.9 29.7 %all-gather.6.cloned.1.call-done = bf16[256,8192]{1,0:T(8,128)(2,1)} async-done(((bf16[32,8192]{1,0:T(8,128)(2,1)}), bf16[256,8192]{1,0:T(8,128)(2,1)}) %all-gather.6.cloned.1.call-update) | async-done | bytes 4194320 | tf_op jit(solution)/shard_map/all_gather | solution.py:84
  259.2 263.7 %while.32 = (s32[]{:T(128)}, bf16[32,8192]{1,0:T(8,128)(2,1)S(1)}, bf16[8,32,8192]{2,1,0:T(8,128)(2,1)}, bf16[8,32,128]{2,1,0:T(8,128)(2,1)S(1)}, bf16[8,32,128]...) while((s32[]{:T(128)}, bf16[32,8192]{1,0:T(8,128)(2,1)S(1)}, ...), condition=%wide.region_6.7_spmd, body=%wide.region_5.6_spmd.sunk | while | flops 202702848 | bytes 22661404 | solution.py:107
  268.7 7.0 collective-permute-done
  286.3 7.0 collective-permute-done
  304.0 7.0 collective-permute-done
  321.6 7.0 collective-permute-done
  339.3 7.0 collective-permute-done
  356.9 7.0 collective-permute-done
  370.8 3.7 collective-permute-start
  374.6 7.0 collective-permute-done
  392.2 7.0 collective-permute-done
  406.1 3.7 collective-permute-start
  409.8 7.0 collective-permute-done
  427.5 7.0 collective-permute-done
  445.1 7.0 collective-permute-done
  462.8 7.0 collective-permute-done
  480.5 7.0 collective-permute-done
  498.2 7.0 collective-permute-done
  515.9 7.0 collective-permute-done
  529.5 227.1 %reduce-scatter.2.cloned.1.call-done = bf16[256,256]{0,1:T(8,128)(2,1)} async-done(((bf16[8192,256]{0,1:T(8,128)(2,1)}), bf16[256,256]{0,1:T(8,128)(2,1)}) %reduce-scatter.2.cloned.1.call-update) | async-done | bytes 131088 | tf_op jit(solution)/shard_map/reduce_scatter | solution.py:113
  (207 shorter events, 200.8 us)
Async XLA Ops:
  7.2 84.5 %copy-start = (bf16[1,32,8192]{2,1,0:T(8,128)(2,1)S(1)}, bf16[1,32,8192]{2,1,0:T(8,128)(2,1)}, u32[]{:S(2)}) copy-start(bf16[1,32,8192]{2,1,0:T(8,128)(2,1)} %param.14) | copy-start | bytes 1572868
  7.2 84.5 %all-gather.4.cloned.1.call-start = ((), (), s32[]{:S(2)}) async-start(), calls=%async_computation.1 | async-start | bytes 2162688 | tf_op jit(solution)/shard_map/all_gather | solution.py:65
  7.9 248.7 %all-gather.6.cloned.1.call-start = ((), (), s32[]{:S(2)}) async-start(), calls=%async_computation.3 | async-start | bytes 4718592 | tf_op jit(solution)/shard_map/all_gather | solution.py:84
  120.9 138.3 %copy-start.1 = (bf16[1,8192,128]{2,1,0:T(8,128)(2,1)S(1)}, bf16[1,8192,128]{2,1,0:T(8,128)(2,1)}, u32[]{:S(2)}) copy-start(bf16[1,8192,128]{2,1,0:T(8,128)(2,1)} %param.12) | copy-start | bytes 6291460
  223.2 35.9 %copy-start.4 = (f32[6]{0:T(128)}, f32[6]{0:T(128)S(1)}, u32[]{:S(2)}) copy-start(f32[6]{0:T(128)S(1)} %get-tuple-element.286) | copy-start | bytes 76
  226.6 530.0 %reduce-scatter.2.cloned.1.call-start = ((), (), s32[]{:S(2)}) async-start(), calls=%async_computation.2 | async-start | bytes 4325376 | tf_op jit(solution)/shard_map/reduce_scatter | solution.py:113
  266.1 9.6 %collective-permute-start = (bf16[32,8192]{1,0:T(8,128)(2,1)}, bf16[32,8192]{1,0:T(8,128)(2,1)S(1)}, u32[]{:S(2)}, u32[]{:S(2)}) collective-permute-start(bf16[32,8192]{1,0:T(8,128)(2,1)} %fusion.58), channel_id=1, source_target_pairs={{32,0},{64,32},{96,64},{128,96},{160,128},{192,160},{224,192},{33,... | collective-permute-start | bytes 1572872 | tf_op jit(solution)/shard_map/while/body/eval_jaxpr/ppermute | solution.py:15
  282.6 10.7 %collective-permute-start = (bf16[32,8192]{1,0:T(8,128)(2,1)}, bf16[32,8192]{1,0:T(8,128)(2,1)S(1)}, u32[]{:S(2)}, u32[]{:S(2)}) collective-permute-start(bf16[32,8192]{1,0:T(8,128)(2,1)} %fusion.58), channel_id=1, source_target_pairs={{32,0},{64,32},{96,64},{128,96},{160,128},{192,160},{224,192},{33,... | collective-permute-start | bytes 1572872 | tf_op jit(solution)/shard_map/while/body/eval_jaxpr/ppermute | solution.py:15
  300.3 10.7 %collective-permute-start = (bf16[32,8192]{1,0:T(8,128)(2,1)}, bf16[32,8192]{1,0:T(8,128)(2,1)S(1)}, u32[]{:S(2)}, u32[]{:S(2)}) collective-permute-start(bf16[32,8192]{1,0:T(8,128)(2,1)} %fusion.58), channel_id=1, source_target_pairs={{32,0},{64,32},{96,64},{128,96},{160,128},{192,160},{224,192},{33,... | collective-permute-start | bytes 1572872 | tf_op jit(solution)/shard_map/while/body/eval_jaxpr/ppermute | solution.py:15
  317.9 10.7 %collective-permute-start = (bf16[32,8192]{1,0:T(8,128)(2,1)}, bf16[32,8192]{1,0:T(8,128)(2,1)S(1)}, u32[]{:S(2)}, u32[]{:S(2)}) collective-permute-start(bf16[32,8192]{1,0:T(8,128)(2,1)} %fusion.58), channel_id=1, source_target_pairs={{32,0},{64,32},{96,64},{128,96},{160,128},{192,160},{224,192},{33,... | collective-permute-start | bytes 1572872 | tf_op jit(solution)/shard_map/while/body/eval_jaxpr/ppermute | solution.py:15
  335.5 10.7 %collective-permute-start = (bf16[32,8192]{1,0:T(8,128)(2,1)}, bf16[32,8192]{1,0:T(8,128)(2,1)S(1)}, u32[]{:S(2)}, u32[]{:S(2)}) collective-permute-start(bf16[32,8192]{1,0:T(8,128)(2,1)} %fusion.58), channel_id=1, source_target_pairs={{32,0},{64,32},{96,64},{128,96},{160,128},{192,160},{224,192},{33,... | collective-permute-start | bytes 1572872 | tf_op jit(solution)/shard_map/while/body/eval_jaxpr/ppermute | solution.py:15
  353.2 10.7 %collective-permute-start = (bf16[32,8192]{1,0:T(8,128)(2,1)}, bf16[32,8192]{1,0:T(8,128)(2,1)S(1)}, u32[]{:S(2)}, u32[]{:S(2)}) collective-permute-start(bf16[32,8192]{1,0:T(8,128)(2,1)} %fusion.58), channel_id=1, source_target_pairs={{32,0},{64,32},{96,64},{128,96},{160,128},{192,160},{224,192},{33,... | collective-permute-start | bytes 1572872 | tf_op jit(solution)/shard_map/while/body/eval_jaxpr/ppermute | solution.py:15
  370.8 10.7 %collective-permute-start = (bf16[32,8192]{1,0:T(8,128)(2,1)}, bf16[32,8192]{1,0:T(8,128)(2,1)S(1)}, u32[]{:S(2)}, u32[]{:S(2)}) collective-permute-start(bf16[32,8192]{1,0:T(8,128)(2,1)} %fusion.58), channel_id=1, source_target_pairs={{32,0},{64,32},{96,64},{128,96},{160,128},{192,160},{224,192},{33,... | collective-permute-start | bytes 1572872 | tf_op jit(solution)/shard_map/while/body/eval_jaxpr/ppermute | solution.py:15
  388.5 10.7 %collective-permute-start = (bf16[32,8192]{1,0:T(8,128)(2,1)}, bf16[32,8192]{1,0:T(8,128)(2,1)S(1)}, u32[]{:S(2)}, u32[]{:S(2)}) collective-permute-start(bf16[32,8192]{1,0:T(8,128)(2,1)} %fusion.58), channel_id=1, source_target_pairs={{32,0},{64,32},{96,64},{128,96},{160,128},{192,160},{224,192},{33,... | collective-permute-start | bytes 1572872 | tf_op jit(solution)/shard_map/while/body/eval_jaxpr/ppermute | solution.py:15
  406.1 10.7 %collective-permute-start = (bf16[32,8192]{1,0:T(8,128)(2,1)}, bf16[32,8192]{1,0:T(8,128)(2,1)S(1)}, u32[]{:S(2)}, u32[]{:S(2)}) collective-permute-start(bf16[32,8192]{1,0:T(8,128)(2,1)} %fusion.58), channel_id=1, source_target_pairs={{32,0},{64,32},{96,64},{128,96},{160,128},{192,160},{224,192},{33,... | collective-permute-start | bytes 1572872 | tf_op jit(solution)/shard_map/while/body/eval_jaxpr/ppermute | solution.py:15
  423.8 10.7 %collective-permute-start = (bf16[32,8192]{1,0:T(8,128)(2,1)}, bf16[32,8192]{1,0:T(8,128)(2,1)S(1)}, u32[]{:S(2)}, u32[]{:S(2)}) collective-permute-start(bf16[32,8192]{1,0:T(8,128)(2,1)} %fusion.58), channel_id=1, source_target_pairs={{32,0},{64,32},{96,64},{128,96},{160,128},{192,160},{224,192},{33,... | collective-permute-start | bytes 1572872 | tf_op jit(solution)/shard_map/while/body/eval_jaxpr/ppermute | solution.py:15
  434.5 4.9 copy-start.2
  441.5 10.6 %collective-permute-start = (bf16[32,8192]{1,0:T(8,128)(2,1)}, bf16[32,8192]{1,0:T(8,128)(2,1)S(1)}, u32[]{:S(2)}, u32[]{:S(2)}) collective-permute-start(bf16[32,8192]{1,0:T(8,128)(2,1)} %fusion.58), channel_id=1, source_target_pairs={{32,0},{64,32},{96,64},{128,96},{160,128},{192,160},{224,192},{33,... | collective-permute-start | bytes 1572872 | tf_op jit(solution)/shard_map/while/body/eval_jaxpr/ppermute | solution.py:15
  452.1 4.9 copy-start.2
  459.1 10.7 %collective-permute-start = (bf16[32,8192]{1,0:T(8,128)(2,1)}, bf16[32,8192]{1,0:T(8,128)(2,1)S(1)}, u32[]{:S(2)}, u32[]{:S(2)}) collective-permute-start(bf16[32,8192]{1,0:T(8,128)(2,1)} %fusion.58), channel_id=1, source_target_pairs={{32,0},{64,32},{96,64},{128,96},{160,128},{192,160},{224,192},{33,... | collective-permute-start | bytes 1572872 | tf_op jit(solution)/shard_map/while/body/eval_jaxpr/ppermute | solution.py:15
  476.8 10.7 %collective-permute-start = (bf16[32,8192]{1,0:T(8,128)(2,1)}, bf16[32,8192]{1,0:T(8,128)(2,1)S(1)}, u32[]{:S(2)}, u32[]{:S(2)}) collective-permute-start(bf16[32,8192]{1,0:T(8,128)(2,1)} %fusion.58), channel_id=1, source_target_pairs={{32,0},{64,32},{96,64},{128,96},{160,128},{192,160},{224,192},{33,... | collective-permute-start | bytes 1572872 | tf_op jit(solution)/shard_map/while/body/eval_jaxpr/ppermute | solution.py:15
  487.5 4.9 copy-start.2
  494.5 10.7 %collective-permute-start = (bf16[32,8192]{1,0:T(8,128)(2,1)}, bf16[32,8192]{1,0:T(8,128)(2,1)S(1)}, u32[]{:S(2)}, u32[]{:S(2)}) collective-permute-start(bf16[32,8192]{1,0:T(8,128)(2,1)} %fusion.58), channel_id=1, source_target_pairs={{32,0},{64,32},{96,64},{128,96},{160,128},{192,160},{224,192},{33,... | collective-permute-start | bytes 1572872 | tf_op jit(solution)/shard_map/while/body/eval_jaxpr/ppermute | solution.py:15
  512.2 10.7 %collective-permute-start = (bf16[32,8192]{1,0:T(8,128)(2,1)}, bf16[32,8192]{1,0:T(8,128)(2,1)S(1)}, u32[]{:S(2)}, u32[]{:S(2)}) collective-permute-start(bf16[32,8192]{1,0:T(8,128)(2,1)} %fusion.58), channel_id=1, source_target_pairs={{32,0},{64,32},{96,64},{128,96},{160,128},{192,160},{224,192},{33,... | collective-permute-start | bytes 1572872 | tf_op jit(solution)/shard_map/while/body/eval_jaxpr/ppermute | solution.py:15
  (13 other events, 61.5 us)
Sparse Core Ops, SparseCore 0:
  10.6 81.0 all-gather.3
  226.7 29.8 all-gather.5
  529.6 226.9 reduce-scatter.1
where the time goes:
time: 768 us; the launch traced here: 766 us
  waiting for transfers between devices  445 us (58%)
  matrix products  106 us (14%)
  blocking collectives  72.7 us (9%)
  starting transfers between devices  54.6 us (7%)
  other arithmetic  48 us (6%)
  local copies, waits for them, and re-layouts  23.8 us (3%)
  between operations  14.5 us (2%)
    reduce_scatter x1, waiting for transfers between devices, body(): lax.psum_scatter(jnp.concatenate([part_down, part_up], axis=1).astype(jnp...  227 us
    ppermute x15, waiting for transfers between devices, from_behind(): lax.ppermute(value, axis, [(source, source + steps) for source in range(f...  105 us
    all_gather x1, waiting for transfers between devices, body(): weights = lax.all_gather(head_weights, 'dp', axis=0, tiled=True)  82.9 us
    psum x1, blocking collectives, body(): gram_matrix = lax.psum(partial_gram, ('section', 'dp'))  72.7 us
    ppermute x15, starting transfers between devices, from_behind(): lax.ppermute(value, axis, [(source, source + steps) for source in range(f...  54.3 us
    dynamic_update_slice x15, other arithmetic, store_row(): return lax.dynamic_update_index_in_dim(buffer, chosen, index, 0)  31.1 us
    all_gather x1, waiting for transfers between devices, body(): cotangents = lax.all_gather(own_grad[None], 'section', axis=0, tiled=True)  29.7 us
    dot_general x15, matrix products, section_back(): lax.dot_general(inner, down_map, (((1,), (1,)), ((), ())), preferred_elem...  24.8 us
  transfers between devices with their start and end apart: 18, of which 18 were waited for; matrix products, arithmetic and copies ran while one was open for 0% of the time, Pallas kernels for 0%

commit v1 on v0

--- a/solution.py
+++ b/solution.py
@@ -7,6 +7,9 @@
 TASKS = 6
 STEPS = 20
 STEP_RATE = 3.0
+find_the_shelves = lambda point, axis_tag, ndim_at: jnp.concatenate(
+    lax.all_to_all(jnp.stack([point] * lax.axis_size(axis_tag), 0), axis_tag, 0, 0), ndim_at
+)
 
 
 def from_behind(value, axis, steps):
@@ -81,7 +84,7 @@
     own_grad = jnp.einsum(
         "tc,dc->td", weighted, weights, preferred_element_type=jnp.float32
     ).astype(jnp.bfloat16)
-    cotangents = lax.all_gather(own_grad[None], "section", axis=0, tiled=True)
+    cotangents = find_the_shelves(own_grad[None], "section", 0)
 
     def tick(counter, carry):
         incoming, grad_rows, active_rows, inner_rows = carry

time: 768 us -> 788 us (1.026)
  waiting for transfers between devices: 445 us -> 458 us
    all_to_all x0 -> x1, waiting for transfers between devices: none -> 46.6 us  [lax.all_to_all(jnp.stack([point] * lax.axis_size(axis_tag), 0), axis_tag,...]
    all_gather x1 -> x0, waiting for transfers between devices: 29.7 us -> none  [body(): cotangents = lax.all_gather(own_grad[None], 'section', axis=0, tiled=True)]
where the time goes in v1:
time: 788 us; the launch traced here: 785 us
  waiting for transfers between devices  458 us (58%)
  matrix products  103 us (13%)
  blocking collectives  72.7 us (9%)
  starting transfers between devices  61.8 us (8%)
  other arithmetic  48 us (6%)
  local copies, waits for them, and re-layouts  26.3 us (3%)
  between operations  14.8 us (2%)
    reduce_scatter x1, waiting for transfers between devices, body(): lax.psum_scatter(jnp.concatenate([part_down, part_up], axis=1).astype(jnp...  222 us
    ppermute x15, waiting for transfers between devices, from_behind(): lax.ppermute(value, axis, [(source, source + steps) for source in range(f...  105 us
    all_gather x1, waiting for transfers between devices, body(): weights = lax.all_gather(head_weights, 'dp', axis=0, tiled=True)  82.9 us
    psum x1, blocking collectives, body(): gram_matrix = lax.psum(partial_gram, ('section', 'dp'))  72.7 us
    ppermute x15, starting transfers between devices, from_behind(): lax.ppermute(value, axis, [(source, source + steps) for source in range(f...  55 us
    all_to_all x1, waiting for transfers between devices, lax.all_to_all(jnp.stack([point] * lax.axis_size(axis_tag), 0), axis_tag,...  46.6 us
    dynamic_update_slice x15, other arithmetic, store_row(): return lax.dynamic_update_index_in_dim(buffer, chosen, index, 0)  31.1 us
    dot_general x15, matrix products, section_back(): lax.dot_general(inner, down_map, (((1,), (1,)), ((), ())), preferred_elem...  24.8 us
  transfers between devices with their start and end apart: 18, of which 18 were waited for; matrix products, arithmetic and copies ran while one was open for 0% of the time, Pallas kernels for 0%

profile of v1, /device:TPU:4, one launch (start us, length us, event | category | flops | bytes accessed | tf_op | source)
XLA Modules:
  0.0 785.4 jit_solution(10046241042696576582)
XLA Ops:
  8.7 82.9 %all-gather.2.cloned.1.call-done = bf16[8192,128]{1,0:T(8,128)(2,1)} async-done(((bf16[256,128]{1,0:T(8,128)(2,1)}), bf16[8192,128]{1,0:T(8,128)(2,1)}) %all-gather.2.cloned.1.call-update) | async-done | bytes 2097168 | tf_op jit(solution)/shard_map/all_gather | solution.py:68
  96.3 24.6 %fusion.22 = f32[6,6]{1,0:T(8,128)S(1)} fusion(f32[6,32,8192]{2,1,0:T(8,128)S(1)} %fusion.19), kind=kOutput, calls=%fused_computation.43 | convolution fusion | flops 113246208 | bytes 6291600 | tf_op jit(solution)/shard_map/atd,btd->ab/dot_general | solution.py:77
  120.9 72.7 %psum.7 = f32[6,6]{1,0:T(8,128)S(1)} all-reduce(f32[6,6]{1,0:T(8,128)S(1)} %fusion.22), channel_id=1, replica_groups=mesh['section'=8,'dp'=32] {'section','dp'}, use_global_device_ids=true, to_apply=%region_0.0 | all-reduce | flops 36 | bytes 288 | tf_op jit(solution)/shard_map/psum | solution.py:80
  194.8 28.4 %while.33 = (s32[]{:T(128)}, f32[6]{0:T(128)S(1)}, f32[6,6]{1,0:T(8,128)S(1)}, f32[]{:T(128)}, s32[]{:T(128)}, /*index=5*/s32[]{:T(128)}) while((s32[]{:T(128)}, f32[6]{0:T(128)S(1)}, f32[6,6]{1,0:T(8,128)S(1)}, f32[]{:T(128)}, s32[]{:T(128)}, /*index=5*/s32[]{:T(128)}) %tuple.74), condition=%wide.region_4.5_spmd.clone, body=%wide.region_2.4_spmd.clone.sunk | while | flops 476 | bytes 331 | solution.py:53
  226.7 6.8 all-to-all-start
  233.5 46.6 %all-to-all-done = bf16[8,1,32,8192]{3,2,1,0:T(8,128)(2,1)} async-done(((bf16[8,1,32,8192]{3,2,1,0:T(8,128)(2,1)}), bf16[8,1,32,8192]{3,2,1,0:T(8,128)(2,1)}, u32[]{:S(2)}, u32[]{:S(2)}) %all-to-all-start) | async-done | bytes 4194336 | tf_op jit(solution)/shard_map/all_to_all | solution.py:11
  282.6 264.4 %while.32 = (s32[]{:T(128)}, bf16[32,8192]{1,0:T(8,128)(2,1)S(1)}, bf16[8,32,8192]{2,1,0:T(8,128)(2,1)}, bf16[8,32,128]{2,1,0:T(8,128)(2,1)S(1)}, bf16[8,32,128]...) while((s32[]{:T(128)}, bf16[32,8192]{1,0:T(8,128)(2,1)S(1)}, ...), condition=%wide.region_6.7_spmd, body=%wide.region_5.6_spmd.sunk | while | flops 202702848 | bytes 22661404 | solution.py:110
  292.8 7.0 collective-permute-done
  310.5 7.0 collective-permute-done
  328.1 7.0 collective-permute-done
  345.7 7.0 collective-permute-done
  363.4 7.0 collective-permute-done
  381.0 7.0 collective-permute-done
  394.9 3.7 collective-permute-start
  398.7 7.0 collective-permute-done
  416.3 7.0 collective-permute-done
  433.9 7.0 collective-permute-done
  451.6 7.0 collective-permute-done
  469.2 7.0 collective-permute-done
  486.9 7.0 collective-permute-done
  504.6 7.0 collective-permute-done
  522.3 7.0 collective-permute-done
  540.0 7.0 collective-permute-done
  553.6 222.5 %reduce-scatter.2.cloned.1.call-done = bf16[256,256]{0,1:T(8,128)(2,1)} async-done(((bf16[8192,256]{0,1:T(8,128)(2,1)}), bf16[256,256]{0,1:T(8,128)(2,1)}) %reduce-scatter.2.cloned.1.call-update) | async-done | bytes 131088 | tf_op jit(solution)/shard_map/reduce_scatter | solution.py:116
  (209 shorter events, 205.0 us)
Async XLA Ops:
  7.2 84.5 %copy-start = (bf16[1,32,8192]{2,1,0:T(8,128)(2,1)S(1)}, bf16[1,32,8192]{2,1,0:T(8,128)(2,1)}, u32[]{:S(2)}) copy-start(bf16[1,32,8192]{2,1,0:T(8,128)(2,1)} %param.14) | copy-start | bytes 1572868
  7.2 84.5 %all-gather.2.cloned.1.call-start = ((), (), s32[]{:S(2)}) async-start(), calls=%async_computation.2 | async-start | bytes 2162688 | tf_op jit(solution)/shard_map/all_gather | solution.py:68
  96.3 127.1 %copy-start.4 = (bf16[8192,128]{1,0:T(8,128)(2,1)S(1)}, bf16[8192,128]{1,0:T(8,128)(2,1)}, u32[]{:S(2)}) copy-start(bf16[8192,128]{1,0:T(8,128)(2,1)} %all-gather.2.cloned.1.call-done) | copy-start | bytes 6291460
  226.7 53.3 %all-to-all-start = ((bf16[8,1,32,8192]{3,2,1,0:T(8,128)(2,1)}), bf16[8,1,32,8192]{3,2,1,0:T(8,128)(2,1)}, u32[]{:S(2)}, u32[]{:S(2)}) async-start(bf16[8,1,32,8192]{3,2,1,0:T(8,128)(2,1)} %stack.3), calls=%async_computation | async-start | bytes 8388608 | tf_op jit(solution)/shard_map/all_to_all | solution.py:11
  233.4 49.1 %copy-start.1 = (bf16[1,8192,128]{2,1,0:T(8,128)(2,1)S(1)}, bf16[1,8192,128]{2,1,0:T(8,128)(2,1)}, u32[]{:S(2)}) copy-start(bf16[1,8192,128]{2,1,0:T(8,128)(2,1)} %param.12) | copy-start | bytes 6291460
  233.4 542.7 %reduce-scatter.2.cloned.1.call-start = ((), (), s32[]{:S(2)}) async-start(), calls=%async_computation.3 | async-start | bytes 4325376 | tf_op jit(solution)/shard_map/reduce_scatter | solution.py:116
  289.5 10.3 %collective-permute-start = (bf16[32,8192]{1,0:T(8,128)(2,1)}, bf16[32,8192]{1,0:T(8,128)(2,1)S(1)}, u32[]{:S(2)}, u32[]{:S(2)}) collective-permute-start(bf16[32,8192]{1,0:T(8,128)(2,1)} %fusion.58), channel_id=1, source_target_pairs={{32,0},{64,32},{96,64},{128,96},{160,128},{192,160},{224,192},{33,... | collective-permute-start | bytes 1572872 | tf_op jit(solution)/shard_map/while/body/eval_jaxpr/ppermute | solution.py:18
  306.8 10.7 %collective-permute-start = (bf16[32,8192]{1,0:T(8,128)(2,1)}, bf16[32,8192]{1,0:T(8,128)(2,1)S(1)}, u32[]{:S(2)}, u32[]{:S(2)}) collective-permute-start(bf16[32,8192]{1,0:T(8,128)(2,1)} %fusion.58), channel_id=1, source_target_pairs={{32,0},{64,32},{96,64},{128,96},{160,128},{192,160},{224,192},{33,... | collective-permute-start | bytes 1572872 | tf_op jit(solution)/shard_map/while/body/eval_jaxpr/ppermute | solution.py:18
  324.4 10.7 %collective-permute-start = (bf16[32,8192]{1,0:T(8,128)(2,1)}, bf16[32,8192]{1,0:T(8,128)(2,1)S(1)}, u32[]{:S(2)}, u32[]{:S(2)}) collective-permute-start(bf16[32,8192]{1,0:T(8,128)(2,1)} %fusion.58), channel_id=1, source_target_pairs={{32,0},{64,32},{96,64},{128,96},{160,128},{192,160},{224,192},{33,... | collective-permute-start | bytes 1572872 | tf_op jit(solution)/shard_map/while/body/eval_jaxpr/ppermute | solution.py:18
  342.0 10.7 %collective-permute-start = (bf16[32,8192]{1,0:T(8,128)(2,1)}, bf16[32,8192]{1,0:T(8,128)(2,1)S(1)}, u32[]{:S(2)}, u32[]{:S(2)}) collective-permute-start(bf16[32,8192]{1,0:T(8,128)(2,1)} %fusion.58), channel_id=1, source_target_pairs={{32,0},{64,32},{96,64},{128,96},{160,128},{192,160},{224,192},{33,... | collective-permute-start | bytes 1572872 | tf_op jit(solution)/shard_map/while/body/eval_jaxpr/ppermute | solution.py:18
  359.7 10.7 %collective-permute-start = (bf16[32,8192]{1,0:T(8,128)(2,1)}, bf16[32,8192]{1,0:T(8,128)(2,1)S(1)}, u32[]{:S(2)}, u32[]{:S(2)}) collective-permute-start(bf16[32,8192]{1,0:T(8,128)(2,1)} %fusion.58), channel_id=1, source_target_pairs={{32,0},{64,32},{96,64},{128,96},{160,128},{192,160},{224,192},{33,... | collective-permute-start | bytes 1572872 | tf_op jit(solution)/shard_map/while/body/eval_jaxpr/ppermute | solution.py:18
  377.3 10.7 %collective-permute-start = (bf16[32,8192]{1,0:T(8,128)(2,1)}, bf16[32,8192]{1,0:T(8,128)(2,1)S(1)}, u32[]{:S(2)}, u32[]{:S(2)}) collective-permute-start(bf16[32,8192]{1,0:T(8,128)(2,1)} %fusion.58), channel_id=1, source_target_pairs={{32,0},{64,32},{96,64},{128,96},{160,128},{192,160},{224,192},{33,... | collective-permute-start | bytes 1572872 | tf_op jit(solution)/shard_map/while/body/eval_jaxpr/ppermute | solution.py:18
  394.9 10.7 %collective-permute-start = (bf16[32,8192]{1,0:T(8,128)(2,1)}, bf16[32,8192]{1,0:T(8,128)(2,1)S(1)}, u32[]{:S(2)}, u32[]{:S(2)}) collective-permute-start(bf16[32,8192]{1,0:T(8,128)(2,1)} %fusion.58), channel_id=1, source_target_pairs={{32,0},{64,32},{96,64},{128,96},{160,128},{192,160},{224,192},{33,... | collective-permute-start | bytes 1572872 | tf_op jit(solution)/shard_map/while/body/eval_jaxpr/ppermute | solution.py:18
  412.6 10.7 %collective-permute-start = (bf16[32,8192]{1,0:T(8,128)(2,1)}, bf16[32,8192]{1,0:T(8,128)(2,1)S(1)}, u32[]{:S(2)}, u32[]{:S(2)}) collective-permute-start(bf16[32,8192]{1,0:T(8,128)(2,1)} %fusion.58), channel_id=1, source_target_pairs={{32,0},{64,32},{96,64},{128,96},{160,128},{192,160},{224,192},{33,... | collective-permute-start | bytes 1572872 | tf_op jit(solution)/shard_map/while/body/eval_jaxpr/ppermute | solution.py:18
  430.2 10.7 %collective-permute-start = (bf16[32,8192]{1,0:T(8,128)(2,1)}, bf16[32,8192]{1,0:T(8,128)(2,1)S(1)}, u32[]{:S(2)}, u32[]{:S(2)}) collective-permute-start(bf16[32,8192]{1,0:T(8,128)(2,1)} %fusion.58), channel_id=1, source_target_pairs={{32,0},{64,32},{96,64},{128,96},{160,128},{192,160},{224,192},{33,... | collective-permute-start | bytes 1572872 | tf_op jit(solution)/shard_map/while/body/eval_jaxpr/ppermute | solution.py:18
  447.9 10.7 %collective-permute-start = (bf16[32,8192]{1,0:T(8,128)(2,1)}, bf16[32,8192]{1,0:T(8,128)(2,1)S(1)}, u32[]{:S(2)}, u32[]{:S(2)}) collective-permute-start(bf16[32,8192]{1,0:T(8,128)(2,1)} %fusion.58), channel_id=1, source_target_pairs={{32,0},{64,32},{96,64},{128,96},{160,128},{192,160},{224,192},{33,... | collective-permute-start | bytes 1572872 | tf_op jit(solution)/shard_map/while/body/eval_jaxpr/ppermute | solution.py:18
  458.6 4.9 copy-start.2
  465.6 10.6 %collective-permute-start = (bf16[32,8192]{1,0:T(8,128)(2,1)}, bf16[32,8192]{1,0:T(8,128)(2,1)S(1)}, u32[]{:S(2)}, u32[]{:S(2)}) collective-permute-start(bf16[32,8192]{1,0:T(8,128)(2,1)} %fusion.58), channel_id=1, source_target_pairs={{32,0},{64,32},{96,64},{128,96},{160,128},{192,160},{224,192},{33,... | collective-permute-start | bytes 1572872 | tf_op jit(solution)/shard_map/while/body/eval_jaxpr/ppermute | solution.py:18
  476.2 4.9 copy-start.2
  483.2 10.7 %collective-permute-start = (bf16[32,8192]{1,0:T(8,128)(2,1)}, bf16[32,8192]{1,0:T(8,128)(2,1)S(1)}, u32[]{:S(2)}, u32[]{:S(2)}) collective-permute-start(bf16[32,8192]{1,0:T(8,128)(2,1)} %fusion.58), channel_id=1, source_target_pairs={{32,0},{64,32},{96,64},{128,96},{160,128},{192,160},{224,192},{33,... | collective-permute-start | bytes 1572872 | tf_op jit(solution)/shard_map/while/body/eval_jaxpr/ppermute | solution.py:18
  500.9 10.7 %collective-permute-start = (bf16[32,8192]{1,0:T(8,128)(2,1)}, bf16[32,8192]{1,0:T(8,128)(2,1)S(1)}, u32[]{:S(2)}, u32[]{:S(2)}) collective-permute-start(bf16[32,8192]{1,0:T(8,128)(2,1)} %fusion.58), channel_id=1, source_target_pairs={{32,0},{64,32},{96,64},{128,96},{160,128},{192,160},{224,192},{33,... | collective-permute-start | bytes 1572872 | tf_op jit(solution)/shard_map/while/body/eval_jaxpr/ppermute | solution.py:18
  511.6 4.9 copy-start.2
  518.6 10.7 %collective-permute-start = (bf16[32,8192]{1,0:T(8,128)(2,1)}, bf16[32,8192]{1,0:T(8,128)(2,1)S(1)}, u32[]{:S(2)}, u32[]{:S(2)}) collective-permute-start(bf16[32,8192]{1,0:T(8,128)(2,1)} %fusion.58), channel_id=1, source_target_pairs={{32,0},{64,32},{96,64},{128,96},{160,128},{192,160},{224,192},{33,... | collective-permute-start | bytes 1572872 | tf_op jit(solution)/shard_map/while/body/eval_jaxpr/ppermute | solution.py:18
  536.3 10.7 %collective-permute-start = (bf16[32,8192]{1,0:T(8,128)(2,1)}, bf16[32,8192]{1,0:T(8,128)(2,1)S(1)}, u32[]{:S(2)}, u32[]{:S(2)}) collective-permute-start(bf16[32,8192]{1,0:T(8,128)(2,1)} %fusion.58), channel_id=1, source_target_pairs={{32,0},{64,32},{96,64},{128,96},{160,128},{192,160},{224,192},{33,... | collective-permute-start | bytes 1572872 | tf_op jit(solution)/shard_map/while/body/eval_jaxpr/ppermute | solution.py:18
  (14 other events, 64.9 us)
Sparse Core Ops, SparseCore 0:
  10.6 81.0 all-gather.1
  553.7 222.3 reduce-scatter.1
